TPU v7x, 32 devices: a whole 2x2x4 slice. The times are simulated.
32 devices in a mesh: grp: 4 (over y, core), blk: 8 (over z, x).
Axes of the slice: x: 2, y: 2, z: 4, core: 2. Of those that a mesh axis runs over, the one named last changes fastest.
Arguments:
- features: bfloat16 [4096, 128], P(('grp', 'blk')), may hold values from -6 to 6
- col_scale: float32 [4096], P(('grp', 'blk')), may hold values from 0.5 to 2
- row_scale: float32 [4096], P(('grp', 'blk')), may hold values from 0.5 to 2
- tiles: bfloat16 [1024, 128, 128], P(('grp', 'blk')), may hold values from 0 to 0.03125
- tile_cols: int32 [1024], P(('grp', 'blk')), may hold values from 0 to 3
- weight: bfloat16 [128, 256], replicated, may hold values from -0.5 to 0.5
- cotangent: bfloat16 [4096, 256], P(('grp', 'blk')), may hold values from -0.1875 to 0.1875
- train_mask: int32 [4096], P(('grp', 'blk')), may hold values 0 or 1
Outputs:
- hidden: bfloat16 [4096, 256], P(('grp', 'blk'))
- weight_grad: float32 [128, 256], replicated
All inputs are finite; a program needn't handle non-finite values. No bound on the sum of `train_mask` on one device may be relied on, other than what follows from the above.
Results may differ from a plain program's by a relative error of at most 0.0054.
Values may be sent and summed in bfloat16 or wider, within the bound.
A program may use at most 128 MiB of HBM per device.

v0:
```python
import jax
import jax.numpy as jnp
from jax import lax
from jax.sharding import PartitionSpec as P

TPR = 4


def activate(values):
    return jax.nn.gelu(values, approximate=True)


def shards(features, col_scale, row_scale, tiles, tile_cols, weight, cotangent, train_mask):
    node_dev = features.shape[0]
    fin_width = features.shape[1]
    tile = tiles.shape[1]
    per_dev = node_dev // tile
    grp_count = lax.axis_size("grp")
    blk_count = lax.axis_size("blk")
    scaled = (col_scale[:, None] * features.astype(jnp.float32)).astype(jnp.bfloat16)
    moved_tiles, moved_cols = (
        lax.all_to_all(tiles, "blk", split_axis=0, concat_axis=0, tiled=True),
        lax.all_to_all(tile_cols, "blk", split_axis=0, concat_axis=0, tiled=True),
    )
    everything = lax.all_gather(scaled, ("grp", "blk"), axis=0, tiled=True)
    everything = everything.reshape(grp_count * blk_count * per_dev, tile, fin_width)
    cols_view = moved_cols.reshape(blk_count, per_dev * TPR)
    colset = jnp.arange(blk_count, dtype=jnp.int32)[:, None]
    global_cols = (cols_view // per_dev * blk_count + colset) * per_dev + cols_view % per_dev
    picked = jnp.take(everything, global_cols.reshape(-1), axis=0)
    picked = picked.reshape(blk_count, per_dev, TPR, tile, fin_width)
    piece = moved_tiles.reshape(blk_count, per_dev, TPR, tile, tile)
    aggregate = jnp.einsum("bpkij,bpkjf->pif", piece, picked, preferred_element_type=jnp.float32)
    aggregate = aggregate.reshape(node_dev, fin_width)
    mixed = row_scale[:, None] * aggregate
    pre = jnp.dot(mixed, weight.astype(jnp.float32), precision=lax.Precision.HIGHEST)
    hidden, backward = jax.vjp(activate, pre)
    masked_grad = cotangent.astype(jnp.float32) * train_mask.astype(jnp.float32)[:, None]
    delta = backward(masked_grad)[0]
    local_grad = jnp.dot(mixed.T, delta, precision=lax.Precision.HIGHEST)
    weight_grad = lax.psum(local_grad, ("grp", "blk"))
    return (hidden.astype(jnp.bfloat16), weight_grad)


def solution(mesh):
    in_specs = (
        P(("grp", "blk"), None),
        P(("grp", "blk")),
        P(("grp", "blk")),
        P(("grp", "blk"), None, None),
        P(("grp", "blk")),
        P(),
        P(("grp", "blk"), None),
        P(("grp", "blk")),
    )
    out_specs = (P(("grp", "blk"), None), P())
    return jax.shard_map(shards, mesh=mesh, in_specs=in_specs, out_specs=out_specs, check_vma=False)
```

profile of v0, /device:TPU:0, one launch (start us, length us, event | category | flops | bytes accessed | tf_op | source)
XLA Modules:
  0.0 208.8 jit_solution(1757387805213414297)
XLA Ops:
  7.2 0.0 copy-start
  7.2 0.0 all-gather.2.cloned.1.call-start
  7.2 1.5 multiply_convert_fusion.1
  8.7 0.0 copy-start.1
  8.7 0.0 all-gather.2.cloned.1.call-update
  8.7 0.6 copy-done.1
  9.3 0.1 all_to_all.9
  9.4 13.5 %all_to_all.14 = s32[8,4,1]{1,2,0:T(1,128)S(1)} all-to-all(s32[8,4,1]{1,2,0:T(1,128)S(1)} %bitcast.25), channel_id=1, replica_groups=mesh['grp'=4,'blk'=8] {'blk'}, dimensions={0} | all-to-all | bytes 256 | tf_op jit(solution)/shard_map/all_to_all | solution.py:23
  22.9 3.6 %all-to-all-start.1 = ((bf16[32,128,128]{2,1,0:T(8,128)(2,1)}), bf16[32,128,128]{2,1,0:T(8,128)(2,1)S(1)}, u32[]{:S(2)}, u32[]{:S(2)}) async-start(bf16[32,128,128]{2,1,0:T(8,128)(2,1)} %param.11), calls=%async_computation.1 | async-start | bytes 2097152 | tf_op jit(solution)/shard_map/all_to_all | solution.py:22
  26.5 0.0 all-reduce.2.cloned.1.call-start
  26.6 0.0 copy-start.3
  26.6 0.1 add.82
  26.6 0.6 copy-done.3
  27.2 0.1 mul.98
  27.3 0.1 copy.17
  27.4 0.1 copy.18
  27.5 45.2 %all-gather.2.cloned.1.call-done = bf16[4096,128]{1,0:T(8,128)(2,1)} async-done(((bf16[128,128]{1,0:T(8,128)(2,1)}), bf16[4096,128]{1,0:T(8,128)(2,1)}) %all-gather.2.cloned.1.call-update) | async-done | bytes 1048592 | tf_op jit(solution)/shard_map/all_gather | solution.py:25
  72.8 2.0 gather_fusion
  74.8 0.7 copy.19
  75.4 0.0 all-to-all-done.1
  75.4 0.0 copy-start.4
  75.4 0.6 copy-done.4
  76.1 0.5 fusion
  76.6 0.0 copy-done
  76.6 0.0 copy-start.2
  76.6 0.9 multiply_convert_fusion
  77.5 0.0 copy-done.2
  77.5 1.0 fusion.10
  78.6 0.0 all-reduce.2.cloned.1.call-update
  78.6 121.8 %all-reduce.2.cloned.1.call-done = f32[128,256]{1,0:T(8,128)} async-done(((f32[128,256]{1,0:T(8,128)}), f32[128,256]{1,0:T(8,128)}) %all-reduce.2.cloned.1.call-update) | async-done | bytes 131088 | tf_op jit(solution)/shard_map/psum | solution.py:41
  200.4 1.6 copy.22
  (6 shorter events, 0.0 us)
Async XLA Ops:
  7.2 69.4 %copy-start = (bf16[128,256]{1,0:T(8,128)(2,1)S(1)}, bf16[128,256]{1,0:T(8,128)(2,1)}, u32[]{:S(2)}) copy-start(bf16[128,256]{1,0:T(8,128)(2,1)} %param.13) | copy-start | bytes 196612
  7.2 65.6 %all-gather.2.cloned.1.call-start = ((), (), s32[]{:S(2)}) async-start(), calls=%async_computation.2 | async-start | bytes 1081344 | tf_op jit(solution)/shard_map/all_gather | solution.py:25
  8.7 0.7 copy-start.1
  22.9 52.5 %all-to-all-start.1 = ((bf16[32,128,128]{2,1,0:T(8,128)(2,1)}), bf16[32,128,128]{2,1,0:T(8,128)(2,1)S(1)}, u32[]{:S(2)}, u32[]{:S(2)}) async-start(bf16[32,128,128]{2,1,0:T(8,128)(2,1)} %param.11), calls=%async_computation.1 | async-start | bytes 2097152 | tf_op jit(solution)/shard_map/all_to_all | solution.py:22
  26.5 173.9 %all-reduce.2.cloned.1.call-start = ((), (), s32[]{:S(2)}) async-start(), calls=%async_computation.3 | async-start | bytes 262144 | tf_op jit(solution)/shard_map/psum | solution.py:41
  26.6 0.7 copy-start.3
  75.4 0.7 copy-start.4
  76.6 0.9 copy-start.2
Sparse Core Ops, SparseCore 0:
  11.6 61.1 all-gather.1
  78.9 121.4 all-reduce.1
where the time goes:
time: 209 us
  waiting for transfers between devices  167 us (80%)
  between operations  14.1 us (7%)
  blocking collectives  13.5 us (6%)
  local copies, waits for them, and re-layouts  6.49 us (3%)
  starting transfers between devices  3.64 us (2%)
  matrix products  2.43 us (1%)
    psum x1, waiting for transfers between devices, shards(): weight_grad = lax.psum(local_grad, ('grp', 'blk'))  122 us
    all_gather x1, waiting for transfers between devices, shards(): everything = lax.all_gather(scaled, ('grp', 'blk'), axis=0, tiled=True)  45.2 us
    all_to_all x1, blocking collectives, shards(): lax.all_to_all(tile_cols, 'blk', split_axis=0, concat_axis=0, tiled=True)  13.5 us
  transfers between devices with their start and end apart: 3, of which 2 were waited for; matrix products, arithmetic and copies ran while one was open for 1% of the time, Pallas kernels for 0%

commit v1 on v0

--- a/solution.py
+++ b/solution.py
@@ -38,7 +38,8 @@
     masked_grad = cotangent.astype(jnp.float32) * train_mask.astype(jnp.float32)[:, None]
     delta = backward(masked_grad)[0]
     local_grad = jnp.dot(mixed.T, delta, precision=lax.Precision.HIGHEST)
-    weight_grad = lax.psum(local_grad, ("grp", "blk"))
+    shards_2 = lax.all_gather(local_grad, ("grp", "blk"))
+    weight_grad = jnp.sum(shards_2, axis=0)
     return (hidden.astype(jnp.bfloat16), weight_grad)
 
 

time: 209 us -> 149 us (0.71)
  waiting for transfers between devices: 167 us -> 106 us
  other arithmetic: 1.51 us -> 5.27 us
  local copies, waits for them, and re-layouts: 6.49 us -> 3.73 us
    psum x1 -> x0, waiting for transfers between devices: 122 us -> none  [shards(): weight_grad = lax.psum(local_grad, ('grp', 'blk'))]
    all_gather x0 -> x1, waiting for transfers between devices: none -> 61.2 us  [shards(): shards_2 = lax.all_gather(local_grad, ('grp', 'blk'))]
    unnamed x11 -> x6, local copies, waits for them, and re-layouts: 3.43 us -> 0.02 us
    reduce_sum x0 -> x1, other arithmetic: none -> 3.1 us  [shards(): weight_grad = jnp.sum(shards_2, axis=0)]
  transfers between devices with their start and end apart: 3 -> 3, of which waited for: 2 -> 2; matrix products, arithmetic and copies ran while one was open for 1% -> 2% of each run, Pallas kernels for 0% -> 0%
where the time goes in v1:
time: 149 us
  waiting for transfers between devices  106 us (71%)
  between operations  14.1 us (9%)
  blocking collectives  13.5 us (9%)
  other arithmetic  5.27 us (4%)
  local copies, waits for them, and re-layouts  3.73 us (3%)
  starting transfers between devices  3.64 us (2%)
  matrix products  2.44 us (2%)
    all_gather x1, waiting for transfers between devices, shards(): shards_2 = lax.all_gather(local_grad, ('grp', 'blk'))  61.2 us
    all_gather x1, waiting for transfers between devices, shards(): everything = lax.all_gather(scaled, ('grp', 'blk'), axis=0, tiled=True)  45.1 us
    all_to_all x1, blocking collectives, shards(): lax.all_to_all(tile_cols, 'blk', split_axis=0, concat_axis=0, tiled=True)  13.5 us
    all_to_all x1, starting transfers between devices, shards(): lax.all_to_all(tiles, 'blk', split_axis=0, concat_axis=0, tiled=True)  3.56 us
    reduce_sum x1, other arithmetic, shards(): weight_grad = jnp.sum(shards_2, axis=0)  3.1 us
  transfers between devices with their start and end apart: 3, of which 2 were waited for; matrix products, arithmetic and copies ran while one was open for 2% of the time, Pallas kernels for 0%

profile of v1, /device:TPU:0, one launch (start us, length us, event | category | flops | bytes accessed | tf_op | source)
XLA Modules:
  0.0 149.1 jit_solution(6529033812634187178)
XLA Ops:
  7.2 0.0 copy-start
  7.2 0.0 copy-start.2
  7.2 0.0 all-gather.4.cloned.1.call-start
  7.2 1.5 multiply_convert_fusion.1
  8.7 0.0 all-gather.4.cloned.1.call-update
  8.7 0.7 all_to_all.9
  9.5 13.5 %all_to_all.14 = s32[8,4,1]{1,2,0:T(1,128)S(1)} all-to-all(s32[8,4,1]{1,2,0:T(1,128)S(1)} %bitcast.27), channel_id=1, replica_groups=mesh['grp'=4,'blk'=8] {'blk'}, dimensions={0} | all-to-all | bytes 256 | tf_op jit(solution)/shard_map/all_to_all | solution.py:23
  23.0 3.6 %all-to-all-start.1 = ((bf16[32,128,128]{2,1,0:T(8,128)(2,1)}), bf16[32,128,128]{2,1,0:T(8,128)(2,1)S(1)}, u32[]{:S(2)}, u32[]{:S(2)}) async-start(bf16[32,128,128]{2,1,0:T(8,128)(2,1)} %param.11), calls=%async_computation.1 | async-start | bytes 2097152 | tf_op jit(solution)/shard_map/all_to_all | solution.py:22
  26.5 0.0 copy-start.1
  26.5 0.0 all-gather.6.cloned.1.call-start
  26.6 0.7 convert_element_type.20
  27.3 0.1 add.80
  27.4 0.1 copy.17
  27.5 0.1 copy.18
  27.6 0.1 mul.98
  27.7 45.1 %all-gather.4.cloned.1.call-done = bf16[4096,128]{1,0:T(8,128)(2,1)} async-done(((bf16[128,128]{1,0:T(8,128)(2,1)}), bf16[4096,128]{1,0:T(8,128)(2,1)}) %all-gather.4.cloned.1.call-update) | async-done | bytes 1048592 | tf_op jit(solution)/shard_map/all_gather | solution.py:25
  72.8 2.0 %gather_fusion = bf16[32,128,128]{2,1,0:T(8,128)(2,1)S(1)} fusion(bf16[32,128,128]{2,1,0:T(8,128)(2,1)} %bitcast.24, s32[1024]{0:T(1024)S(1)} %pad_clamp_fusion), kind=kCustom, calls=%fused_computation | custom fusion | bytes 2097280 | tf_op jit(solution)/shard_map/jit(_take)/gather | solution.py:30
  74.8 0.7 copy.19
  75.5 0.0 all-to-all-done.1
  75.5 0.0 copy-done.2
  75.5 0.5 fusion
  76.0 0.0 copy-done
  76.0 0.9 multiply_convert_fusion
  76.9 0.0 copy-done.1
  76.9 1.0 fusion.10
  77.9 0.0 all-gather.6.cloned.1.call-update
  78.0 61.2 %all-gather.6.cloned.1.call-done = f32[4096,256]{1,0:T(8,128)} async-done(((f32[128,256]{1,0:T(8,128)}), f32[4096,256]{1,0:T(8,128)}) %all-gather.6.cloned.1.call-update) | async-done | bytes 4194320 | tf_op jit(solution)/shard_map/all_gather | solution.py:41
  139.2 3.1 %reduce_sum.9 = f32[128,256]{1,0:T(8,128)} reduce(f32[32,128,256]{2,1,0:T(8,128)} %bitcast.23, f32[]{:T(128)} %constant.57.clone.1), dimensions={0}, to_apply=%region_0.1 | reduce | flops 1015808 | bytes 4325380 | tf_op jit(solution)/shard_map/reduce_sum | solution.py:42
  (5 shorter events, 0.0 us)
Async XLA Ops:
  7.2 68.8 %copy-start = (bf16[128,256]{1,0:T(8,128)(2,1)S(1)}, bf16[128,256]{1,0:T(8,128)(2,1)}, u32[]{:S(2)}) copy-start(bf16[128,256]{1,0:T(8,128)(2,1)} %param.13) | copy-start | bytes 196612
  7.2 68.3 %copy-start.2 = (f32[128]{0:T(128)S(1)}, f32[128]{0:T(128)}, u32[]{:S(2)}) copy-start(f32[128]{0:T(128)} %param.10) | copy-start | bytes 1540
  7.2 65.6 %all-gather.4.cloned.1.call-start = ((), (), s32[]{:S(2)}) async-start(), calls=%async_computation.2 | async-start | bytes 1081344 | tf_op jit(solution)/shard_map/all_gather | solution.py:25
  23.0 52.5 %all-to-all-start.1 = ((bf16[32,128,128]{2,1,0:T(8,128)(2,1)}), bf16[32,128,128]{2,1,0:T(8,128)(2,1)S(1)}, u32[]{:S(2)}, u32[]{:S(2)}) async-start(bf16[32,128,128]{2,1,0:T(8,128)(2,1)} %param.11), calls=%async_computation.1 | async-start | bytes 2097152 | tf_op jit(solution)/shard_map/all_to_all | solution.py:22
  26.5 50.4 %copy-start.1 = (bf16[128,256]{1,0:T(8,128)(2,1)S(1)}, bf16[128,256]{1,0:T(8,128)(2,1)}, u32[]{:S(2)}) copy-start(bf16[128,256]{1,0:T(8,128)(2,1)} %param.14) | copy-start | bytes 196612
  26.5 112.6 %all-gather.6.cloned.1.call-start = ((), (), s32[]{:S(2)}) async-start(), calls=%async_computation.3 | async-start | bytes 4325376 | tf_op jit(solution)/shard_map/all_gather | solution.py:41
Sparse Core Ops, SparseCore 0:
  11.6 61.1 all-gather.3
  78.1 61.0 all-gather.5
